TPU v7x, 256 devices: a whole 4x4x8 slice. The times are simulated.
256 devices in a mesh: slab: 32 (over x_hi, z, core), view: 8 (over x_lo, y).
Axes of the slice: x: 4 (x_hi: 2, x_lo: 2; x = x_hi * 2 + x_lo), y: 4, z: 8, core: 2. Of those that a mesh axis runs over, the one named last changes fastest.
Arguments:
- fine_volume: float32 [128, 4096], P('slab'), may hold values from 0 to 1
- coarse_volume: float32 [512, 4096], P('slab'), may hold values from 0 to 1
- fine_rays: bfloat16 [16, 4096, 128], P('view'), may hold values from -0.09375 to 0.09375
- coarse_rays: bfloat16 [16, 4096, 128], P('view'), may hold values from -0.09375 to 0.09375
- fine_axial: bfloat16 [16, 128, 256], P('view', 'slab'), may hold values from -0.3125 to 0.3125
- coarse_axial: bfloat16 [16, 512, 256], P('view', 'slab'), may hold values from -0.21875 to 0.21875
- measured: float32 [256, 16, 128], P('slab', 'view'), may hold values from 0 to 2
- ray_weight: float32 [256, 16, 128], P('slab', 'view'), may hold values from 0.25 to 0.5
- fine_cell_weight: float32 [128, 4096], P('slab'), may hold values from 0.3 to 0.6
- coarse_cell_weight: float32 [512, 4096], P('slab'), may hold values from 0.3 to 0.6
- margin_blocks: int32 [32, 8], P('slab'), may hold values from 0 to 31, as said below
- ray_hits: int32 [16, 32, 8], P('view', 'slab'), may hold values 0 or 1
Outputs:
- fine_result: float32 [128, 4096], P('slab')
- coarse_result: float32 [512, 4096], P('slab')
Inputs may be any that keep to these rules, and one draw needn't show every extreme that they name: `margin_blocks`: each row lists 8 different block numbers.
All inputs are finite; a program needn't handle non-finite values. No bound on the sum of `ray_hits` on one device may be relied on, other than what follows from the above.
Results may differ from a plain program's by a relative error of at most 0.005.
Values may be sent and summed in bfloat16 or wider, within the bound.
A program may use at most 64 MiB of HBM per device.

v0:
```python
import jax
import jax.numpy as jnp
from jax import lax
from jax.sharding import PartitionSpec as P

ITERS = 3
BLOCK = 128


def body(
    fine_volume,
    coarse_volume,
    fine_rays,
    coarse_rays,
    fine_axial,
    coarse_axial,
    measured,
    ray_weight,
    fine_cell_weight,
    coarse_cell_weight,
    margin_blocks,
    ray_hits,
):
    view_count = fine_rays.shape[0]
    detector_rows = fine_axial.shape[2]
    tile_count = ray_hits.shape[2]
    coarse_cells = coarse_volume.shape[1]
    block_ids = jnp.arange(coarse_cells, dtype=jnp.int32) // BLOCK
    listed = jnp.any(margin_blocks[0][:, None] == block_ids[None, :], axis=0)
    keep_mask = jnp.where(listed, 0.0, 1.0).astype(jnp.float32)[None, :]
    hit_rows = jnp.broadcast_to(
        ray_hits[:, 0, :, None], (view_count, tile_count, detector_rows // tile_count)
    )
    hit_rows = hit_rows.reshape(view_count, detector_rows).astype(jnp.bfloat16)
    fine_depth = fine_axial * hit_rows[:, None, :]
    coarse_depth = coarse_axial * hit_rows[:, None, :]
    fine = fine_volume
    coarse = coarse_volume * keep_mask
    whole_measured, whole_weight = (
        lax.all_gather(measured, "slab", axis=0, tiled=True),
        lax.all_gather(ray_weight, "slab", axis=0, tiled=True),
    )
    for iteration in range(ITERS):
        fine_moment = jnp.einsum(
            "zx,vxu->vzu", fine.astype(jnp.bfloat16), fine_rays, preferred_element_type=jnp.float32
        ).astype(jnp.bfloat16)
        coarse_moment = jnp.einsum(
            "zx,vxu->vzu",
            coarse.astype(jnp.bfloat16),
            coarse_rays,
            preferred_element_type=jnp.float32,
        ).astype(jnp.bfloat16)
        total = jnp.einsum(
            "vzw,vzu->wvu", fine_depth, fine_moment, preferred_element_type=jnp.float32
        )
        projection = lax.psum(
            (
                total
                + jnp.einsum(
                    "vzw,vzu->wvu", coarse_depth, coarse_moment, preferred_element_type=jnp.float32
                )
            ).astype(jnp.bfloat16),
            "slab",
        ).astype(jnp.float32)
        residual = (whole_weight * (whole_measured - projection)).astype(jnp.bfloat16)
        fine_spread = jnp.einsum(
            "vzw,wvu->vzu", fine_depth, residual, preferred_element_type=jnp.float32
        ).astype(jnp.bfloat16)
        coarse_spread = jnp.einsum(
            "vzw,wvu->vzu", coarse_depth, residual, preferred_element_type=jnp.float32
        ).astype(jnp.bfloat16)
        fine_term = jnp.einsum(
            "vzu,vxu->zx", fine_spread, fine_rays, preferred_element_type=jnp.float32
        )
        coarse_term = jnp.einsum(
            "vzu,vxu->zx", coarse_spread, coarse_rays, preferred_element_type=jnp.float32
        )
        fine_back, coarse_back = (
            lax.psum(fine_term.astype(jnp.bfloat16), "view").astype(jnp.float32),
            lax.psum(coarse_term.astype(jnp.bfloat16), "view").astype(jnp.float32),
        )
        fine = fine + fine_cell_weight * fine_back
        coarse = (coarse + coarse_cell_weight * coarse_back) * keep_mask
    return (fine, coarse)


def solution(mesh):
    return jax.shard_map(
        body,
        mesh=mesh,
        in_specs=(
            P("slab", None),
            P("slab", None),
            P("view", None, None),
            P("view", None, None),
            P("view", "slab", None),
            P("view", "slab", None),
            P("slab", "view", None),
            P("slab", "view", None),
            P("slab", None),
            P("slab", None),
            P("slab", None),
            P("view", "slab", None),
        ),
        out_specs=(P("slab", None), P("slab", None)),
        check_vma=False,
    )
```

profile of v0, /device:TPU:1, one launch (start us, length us, event | category | flops | bytes accessed | tf_op | source)
XLA Modules:
  0.0 1101.1 jit_solution(4138401398298017130)
XLA Ops:
  7.3 0.8 convert_element_type.156
  8.3 0.8 compare_reduce_fusion
  9.1 2.3 fusion.15
  11.4 1.3 fusion.11
  12.8 46.7 %all_gather.7 = f32[256,2,128]{2,1,0:T(2,128)S(1)} all-gather(f32[8,2,128]{2,1,0:T(2,128)S(1)} %copy-done.19), channel_id=1, replica_groups=mesh['slab'=32,'view'=8] {'slab'}, dimensions={0}, use_global_device_ids=true | all-gather | bytes 270336 | tf_op jit(solution)/shard_map/all_gather | solution.py:40
  59.6 0.1 copy.22
  59.7 37.4 %all_gather.6 = f32[256,2,128]{2,1,0:T(2,128)S(1)} all-gather(f32[8,2,128]{2,1,0:T(2,128)S(1)} %copy-done.20), channel_id=1, replica_groups=mesh['slab'=32,'view'=8] {'slab'}, dimensions={0}, use_global_device_ids=true | all-gather | bytes 270336 | tf_op jit(solution)/shard_map/all_gather | solution.py:41
  97.1 0.1 copy.23
  97.3 165.7 %all-reduce.7.cloned.1.call-done = bf16[256,2,128]{0,2,1:T(8,128)(2,1)} async-done(((bf16[256,2,128]{0,2,1:T(8,128)(2,1)}), bf16[256,2,128]{0,2,1:T(8,128)(2,1)}) %all-reduce.7.cloned.1.call-update) | async-done | bytes 131088 | tf_op jit(solution)/shard_map/psum | solution.py:56
  263.0 0.9 multiply_convert_fusion.2
  264.0 2.4 fusion.3
  266.3 1.4 fusion
  267.7 27.0 %psum.64 = bf16[4,4096]{1,0:T(4,128)(2,1)} all-reduce(bf16[4,4096]{1,0:T(4,128)(2,1)S(1)} %fusion.3), channel_id=1, replica_groups=mesh['slab'=32,'view'=8] {'view'}, use_global_device_ids=true, to_apply=%region_2.3 | all-reduce | flops 16384 | bytes 65536 | tf_op jit(solution)/shard_map/psum | solution.py:79
  294.8 2.3 fusion.17
  297.1 73.8 %all-reduce.9.cloned.1.call-done = bf16[16,4096]{1,0:T(8,128)(2,1)} async-done(((bf16[16,4096]{1,0:T(8,128)(2,1)}), bf16[16,4096]{1,0:T(8,128)(2,1)}) %all-reduce.9.cloned.1.call-update) | async-done | bytes 131088 | tf_op jit(solution)/shard_map/psum | solution.py:80
  370.9 2.2 fusion.10
  373.2 250.9 %all-reduce.11.cloned.1.call-done = bf16[256,2,128]{0,2,1:T(8,128)(2,1)} async-done(((bf16[256,2,128]{0,2,1:T(8,128)(2,1)}), bf16[256,2,128]{0,2,1:T(8,128)(2,1)}) %all-reduce.11.cloned.1.call-update) | async-done | bytes 131088 | tf_op jit(solution)/shard_map/psum | solution.py:56
  624.2 0.9 multiply_convert_fusion.1
  625.1 2.3 fusion.4
  627.5 1.4 fusion.1
  628.9 27.0 %psum.67 = bf16[4,4096]{1,0:T(4,128)(2,1)} all-reduce(bf16[4,4096]{1,0:T(4,128)(2,1)S(1)} %fusion.4), channel_id=1, replica_groups=mesh['slab'=32,'view'=8] {'view'}, use_global_device_ids=true, to_apply=%region_5.6 | all-reduce | flops 16384 | bytes 65536 | tf_op jit(solution)/shard_map/psum | solution.py:79
  655.9 2.4 fusion.19
  658.3 73.7 %all-reduce.13.cloned.1.call-done = bf16[16,4096]{1,0:T(8,128)(2,1)} async-done(((bf16[16,4096]{1,0:T(8,128)(2,1)}), bf16[16,4096]{1,0:T(8,128)(2,1)}) %all-reduce.13.cloned.1.call-update) | async-done | bytes 131088 | tf_op jit(solution)/shard_map/psum | solution.py:80
  732.0 2.3 fusion.9
  734.4 250.8 %all-reduce.15.cloned.1.call-done = bf16[256,2,128]{0,2,1:T(8,128)(2,1)} async-done(((bf16[256,2,128]{0,2,1:T(8,128)(2,1)}), bf16[256,2,128]{0,2,1:T(8,128)(2,1)}) %all-reduce.15.cloned.1.call-update) | async-done | bytes 131088 | tf_op jit(solution)/shard_map/psum | solution.py:56
  985.1 0.9 multiply_convert_fusion
  986.1 2.4 fusion.5
  988.6 1.4 fusion.2
  990.0 26.4 %psum.70 = bf16[4,4096]{1,0:T(4,128)(2,1)S(1)} all-reduce(bf16[4,4096]{1,0:T(4,128)(2,1)S(1)} %fusion.5), channel_id=1, replica_groups=mesh['slab'=32,'view'=8] {'view'}, use_global_device_ids=true, to_apply=%region_8.9 | all-reduce | flops 16384 | bytes 65536 | tf_op jit(solution)/shard_map/psum | solution.py:79
  1016.4 0.7 multiply_add_fusion
  1017.1 75.4 %all-reduce.17.cloned.1.call-done = bf16[16,4096]{1,0:T(8,128)(2,1)} async-done(((bf16[16,4096]{1,0:T(8,128)(2,1)}), bf16[16,4096]{1,0:T(8,128)(2,1)}) %all-reduce.17.cloned.1.call-update) | async-done | bytes 131088 | tf_op jit(solution)/shard_map/psum | solution.py:80
  1092.6 1.7 add_multiply_fusion
  (59 shorter events, 0.6 us)
Async XLA Ops:
  7.2 4.2 copy-start
  7.2 4.2 copy-start.6
  7.2 4.2 copy-start.1
  7.2 255.8 %all-reduce.7.cloned.1.call-start = ((), (), s32[]{:S(2)}) async-start(), calls=%async_computation | async-start | bytes 262144 | tf_op jit(solution)/shard_map/psum | solution.py:56
  8.3 258.1 %copy-start.14 = (bf16[2,256]{1,0:T(2,128)(2,1)}, bf16[2,256]{1,0:T(2,128)(2,1)S(1)}, u32[]{:S(2)}) copy-start(bf16[2,256]{1,0:T(2,128)(2,1)S(1)} %convert_element_type.158) | copy-start | bytes 3076
  9.1 3.7 copy-start.11
  9.1 3.8 copy-start.19
  11.4 48.3 %copy-start.20 = (f32[8,2,128]{2,1,0:T(2,128)S(1)}, f32[8,2,128]{2,1,0:T(2,128)}, u32[]{:S(2)}) copy-start(f32[8,2,128]{2,1,0:T(2,128)} %param.19) | copy-start | bytes 24580
  11.4 252.5 %copy-start.17 = (bf16[2,4,256]{2,1,0:T(4,128)(2,1)S(1)}, bf16[2,4,256]{2,1,0:T(4,128)(2,1)}, u32[]{:S(2)}) copy-start(bf16[2,4,256]{2,1,0:T(4,128)(2,1)} %param.16) | copy-start | bytes 12292
  12.8 358.1 %all-reduce.9.cloned.1.call-start = ((), (), s32[]{:S(2)}) async-start(), calls=%async_computation.1 | async-start | bytes 262144 | tf_op jit(solution)/shard_map/psum | solution.py:80
  263.9 30.8 %copy-start.4 = (f32[4,4096]{1,0:T(4,128)S(1)}, f32[4,4096]{1,0:T(4,128)}, u32[]{:S(2)}) copy-start(f32[4,4096]{1,0:T(4,128)} %param.12) | copy-start | bytes 196612
  264.0 30.8 %copy-start.7 = (f32[4,4096]{1,0:T(4,128)S(1)}, f32[4,4096]{1,0:T(4,128)}, u32[]{:S(2)}) copy-start(f32[4,4096]{1,0:T(4,128)} %param.20) | copy-start | bytes 196612
  266.3 104.6 %copy-start.2 = (f32[16,4096]{1,0:T(8,128)S(1)}, f32[16,4096]{1,0:T(8,128)}, u32[]{:S(2)}) copy-start(f32[16,4096]{1,0:T(8,128)} %param.21) | copy-start | bytes 786436
  294.7 329.4 %all-reduce.11.cloned.1.call-start = ((), (), s32[]{:S(2)}) async-start(), calls=%async_computation.2 | async-start | bytes 262144 | tf_op jit(solution)/shard_map/psum | solution.py:56
  297.1 328.0 %copy-start.15 = (bf16[2,256]{1,0:T(2,128)(2,1)S(1)}, bf16[2,256]{1,0:T(2,128)(2,1)}, u32[]{:S(2)}) copy-start(bf16[2,256]{1,0:T(2,128)(2,1)} %copy-done.14) | copy-start | bytes 3076
  297.1 328.0 %copy-start.18 = (bf16[2,4,256]{2,1,0:T(4,128)(2,1)S(1)}, bf16[2,4,256]{2,1,0:T(4,128)(2,1)}, u32[]{:S(2)}) copy-start(bf16[2,4,256]{2,1,0:T(4,128)(2,1)} %param.16) | copy-start | bytes 12292
  373.2 358.8 %all-reduce.13.cloned.1.call-start = ((), (), s32[]{:S(2)}) async-start(), calls=%async_computation.3 | async-start | bytes 262144 | tf_op jit(solution)/shard_map/psum | solution.py:80
  627.5 104.6 %copy-start.3 = (bf16[16,4096]{1,0:T(8,128)(2,1)S(1)}, bf16[16,4096]{1,0:T(8,128)(2,1)}, u32[]{:S(2)}) copy-start(bf16[16,4096]{1,0:T(8,128)(2,1)} %all-reduce.9.cloned.1.call-done) | copy-start | bytes 393220
  655.9 329.3 %all-reduce.15.cloned.1.call-start = ((), (), s32[]{:S(2)}) async-start(), calls=%async_computation.4 | async-start | bytes 262144 | tf_op jit(solution)/shard_map/psum | solution.py:56
  734.3 254.3 %copy-start.16 = (bf16[2,256]{1,0:T(2,128)(2,1)S(1)}, bf16[2,256]{1,0:T(2,128)(2,1)}, u32[]{:S(2)}) copy-start(bf16[2,256]{1,0:T(2,128)(2,1)} %copy-done.14) | copy-start | bytes 3076
  734.3 358.2 %all-reduce.17.cloned.1.call-start = ((), (), s32[]{:S(2)}) async-start(), calls=%async_computation.5 | async-start | bytes 262144 | tf_op jit(solution)/shard_map/psum | solution.py:80
  986.1 30.3 %copy-start.5 = (f32[4,4096]{1,0:T(4,128)S(1)}, f32[4,4096]{1,0:T(4,128)}, u32[]{:S(2)}) copy-start(f32[4,4096]{1,0:T(4,128)} %param.12) | copy-start | bytes 196612
  986.1 30.3 %copy-start.8 = (f32[4,4096]{1,0:T(4,128)S(1)}, f32[4,4096]{1,0:T(4,128)}, u32[]{:S(2)}) copy-start(f32[4,4096]{1,0:T(4,128)} %param.20) | copy-start | bytes 196612
  986.1 30.3 %copy-start.9 = (bf16[4,4096]{1,0:T(4,128)(2,1)S(1)}, bf16[4,4096]{1,0:T(4,128)(2,1)}, u32[]{:S(2)}) copy-start(bf16[4,4096]{1,0:T(4,128)(2,1)} %psum.64) | copy-start | bytes 98308
  986.1 30.3 %copy-start.13 = (bf16[4,4096]{1,0:T(4,128)(2,1)S(1)}, bf16[4,4096]{1,0:T(4,128)(2,1)}, u32[]{:S(2)}) copy-start(bf16[4,4096]{1,0:T(4,128)(2,1)} %psum.67) | copy-start | bytes 98308
  986.1 106.4 %copy-start.10 = (bf16[16,4096]{1,0:T(8,128)(2,1)S(1)}, bf16[16,4096]{1,0:T(8,128)(2,1)}, u32[]{:S(2)}) copy-start(bf16[16,4096]{1,0:T(8,128)(2,1)} %all-reduce.13.cloned.1.call-done) | copy-start | bytes 393220
  986.1 106.4 %copy-start.12 = (f32[4096]{0:T(1024)S(1)}, f32[4096]{0:T(1024)}, u32[]{:S(2)}) copy-start(f32[4096]{0:T(1024)} %copy-done.11) | copy-start | bytes 49156
Sparse Core Ops, SparseCore 0:
  12.9 250.0 all-reduce.6
  294.9 75.9 all-reduce.8
  374.1 250.0 all-reduce.10
  656.0 75.9 all-reduce.12
  735.1 250.0 all-reduce.14
  1016.5 75.9 all-reduce.16
where the time goes:
time: 1110 us; the launch traced here: 1100 us
  waiting for transfers between devices  890 us (80%)
  blocking collectives  164 us (15%)
  matrix products  24.1 us (2%)
  between operations  14.4 us (1%)
    psum x3, waiting for transfers between devices, body(): lax.psum((total + jnp.einsum('vzw,vzu->wvu', coarse_depth, coarse_moment,...  667 us
    psum x3, waiting for transfers between devices, body(): lax.psum(coarse_term.astype(jnp.bfloat16), 'view').astype(jnp.float32)  223 us
    psum x3, blocking collectives, body(): lax.psum(fine_term.astype(jnp.bfloat16), 'view').astype(jnp.float32)  80.3 us
    all_gather x1, blocking collectives, body(): lax.all_gather(measured, 'slab', axis=0, tiled=True)  46.7 us
    all_gather x1, blocking collectives, body(): lax.all_gather(ray_weight, 'slab', axis=0, tiled=True)  37.4 us
  transfers between devices with their start and end apart: 6, of which 6 were waited for; matrix products, arithmetic and copies ran while one was open for 1% of the time, Pallas kernels for 0%

commit v1 on v0

v1 whole, which is shorter than its diff:
```python
import functools

import jax
import jax.numpy as jnp
from jax import lax
from jax.experimental import pallas as pl
from jax.experimental.pallas import tpu as pltpu
from jax.sharding import PartitionSpec as P

ITERS = 3
BLOCK = 128
F32 = jnp.float32
BF16 = jnp.bfloat16


def dot(a, b):
    return lax.dot_general(a, b, (((1,), (0,)), ((), ())), preferred_element_type=F32)


def dot_nt(a, b):
    return lax.dot_general(a, b, (((1,), (1,)), ((), ())), preferred_element_type=F32)


def kernel(
    n_z,
    n_y,
    n_slab,
    n_view,
    fine_volume,
    coarse_volume,
    fine_rays,
    coarse_rays,
    fine_axial,
    coarse_axial,
    measured,
    ray_weight,
    fine_weight,
    coarse_weight,
    margin_blocks,
    ray_hits,
    fine_out,
    coarse_out,
    rays_f,
    rays_c,
    vol_in,
    vol_f,
    wgt_f,
    vol_c,
    wgt_c,
    depth_send,
    depth_all,
    depth_t,
    depth_chip,
    mw_send,
    mw_all,
    moment_send,
    moment_all,
    spread_send,
    spread_recv,
    back_send,
    back_recv,
    sum_send,
    sum_recv,
    load_sem,
    init_send_sem,
    init_recv_sem,
    moment_send_sem,
    moment_recv_sem,
    spread_send_sem,
    spread_recv_sem,
    back_send_sem,
    back_recv_sem,
    sum_send_sem,
    sum_recv_sem,
):
    slab = lax.axis_index("slab")
    view = lax.axis_index("view")
    core = lax.rem(slab, 2)
    z = lax.rem(slab // 2, n_z)
    x_hi = slab // (2 * n_z)
    n_xhi = n_slab // (2 * n_z)
    y = lax.rem(view, n_y)
    x_lo = view // n_y
    n_xlo = n_view // n_y
    partner = slab + 1 - 2 * core
    cells = coarse_volume.shape[1]
    width = cells // n_view
    tiles = width // 128
    rows_f = fine_volume.shape[0]
    rows_w = measured.shape[0]
    all_w = fine_axial.shape[2]
    n_tile = ray_hits.shape[2]

    loads = []
    for i, (src, dst) in enumerate(
        [
            (coarse_volume, vol_c),
            (coarse_weight, wgt_c),
            (fine_volume, vol_in.at[0]),
            (fine_weight, vol_in.at[1]),
        ]
    ):
        copy = pltpu.make_async_copy(src, dst, load_sem.at[i])
        copy.start()
        loads.append(copy)
    ray_loads = []
    for b in range(n_view):
        part = pl.ds(b * width, width)
        pair = []
        for i, (src, dst) in enumerate([(coarse_rays, rays_c), (fine_rays, rays_f)]):
            copy = pltpu.make_async_copy(
                src.at[:, part, :], dst.at[:, part, :], load_sem.at[4 + 2 * b + i]
            )
            copy.start()
            pair.append(copy)
        ray_loads.append(pair)

    barrier = pltpu.get_barrier_semaphore()

    def greet_slab(i, carry):
        other = lax.rem(slab + 1 + i, n_slab)
        pl.semaphore_signal(barrier, inc=1, device_id={"slab": other}, device_id_type=pl.DeviceIdType.MESH)
        return carry

    def greet_view(i, carry):
        other = lax.rem(view + 1 + i, n_view)
        pl.semaphore_signal(barrier, inc=1, device_id={"view": other}, device_id_type=pl.DeviceIdType.MESH)
        return carry

    lax.fori_loop(0, n_slab - 1, greet_slab, 0)
    lax.fori_loop(0, n_view - 1, greet_view, 0)

    row_tile = lax.broadcasted_iota(jnp.int32, (1, all_w), 1) // (all_w // n_tile)
    for v in range(2):
        hit = jnp.zeros((1, all_w), F32)
        for t in range(n_tile):
            hit = jnp.where(row_tile == t, ray_hits[v, 0, t].astype(F32), hit)
        dc = (coarse_axial[v].astype(F32) * hit).astype(BF16)
        df = fine_axial[v].astype(F32) * hit
        df = jnp.concatenate([df, jnp.zeros((8 - rows_f, all_w), F32)], axis=0)
        depth_send[v, 0] = dc[0:8]
        depth_send[v, 1] = dc[8:16]
        depth_send[v, 2] = df.astype(BF16)
        mw_send[v, 0] = measured[:, v, :]
        mw_send[v, 1] = ray_weight[:, v, :]
    depth_all[slab] = depth_send[core]
    mw_all[slab] = mw_send[core]

    for copy in loads:
        copy.wait()
    block_id = lax.broadcasted_iota(jnp.int32, (1, cells), 1) // BLOCK
    keep = jnp.ones((1, cells), F32)
    for t in range(margin_blocks.shape[1]):
        keep = jnp.where(block_id == margin_blocks[0, t], 0.0, keep)
    vol_c[...] = vol_c[...] * keep
    wgt_c[...] = wgt_c[...] * keep
    for b in range(n_view):
        for j in range(tiles):
            part = slice(b * width + j * 128, b * width + (j + 1) * 128)
            vol_f[b, j * rows_f : (j + 1) * rows_f, :] = vol_in[0, :, part]
            wgt_f[b, j * rows_f : (j + 1) * rows_f, :] = vol_in[1, :, part]

    group = lax.broadcasted_iota(jnp.int32, (16, 128), 0) // rows_f
    masks = [jnp.where(group == j, 1.0, 0.0).astype(F32) for j in range(tiles)]

    def add_moment(b, acc):
        part = pl.ds(pl.multiple_of(b * width, 128), width)
        lhs_c = vol_c[:, part].astype(BF16)
        packed = vol_f[b]
        lhs_f = jnp.concatenate([(packed * m).astype(BF16) for m in masks], axis=1)
        new = []
        for v in range(2):
            new.append(acc[v] + dot(lhs_c, rays_c[v, part, :]))
        for v in range(2):
            new.append(acc[2 + v] + dot(lhs_f, rays_f[v, part, :]))
        return new

    def finish_moment(k, acc):
        for v in range(2):
            mc = acc[v].astype(BF16)
            half = acc[2 + v][0:8] + acc[2 + v][8:16]
            whole = half + pltpu.roll(half, 4, 0)
            moment_send[k, v, 0] = mc[0:8]
            moment_send[k, v, 1] = mc[8:16]
            moment_send[k, v, 2] = whole.astype(BF16)
        moment_all[k, slab] = moment_send[k, core]

    zero = [jnp.zeros((16, 128), F32) for _ in range(4)]
    acc = zero
    for b in range(n_view):
        for copy in ray_loads[b]:
            copy.wait()
        acc = add_moment(b, acc)
    finish_moment(0, acc)

    pl.semaphore_wait(barrier, n_slab + n_view - 2)

    def to_slab(src, dst, send_sem, recv_sem, other):
        return pltpu.make_async_remote_copy(
            src_ref=src,
            dst_ref=dst,
            send_sem=send_sem,
            recv_sem=recv_sem,
            device_id={"slab": other},
            device_id_type=pl.DeviceIdType.MESH,
        )

    n_chip = n_xhi * n_z

    def each_slab(send):
        def step(i, carry):
            turn = lax.rem(i, n_z)
            half = (turn + 1) // 2
            dz = n_z // 2 + half * (2 * lax.rem(turn, 2) - 1)
            dx = n_xhi - 1 - i // n_z
            chip = lax.rem(x_hi + dx, n_xhi) * n_z + lax.rem(z + dz + n_z, n_z)
            for c in range(2):
                send(2 * chip + c, c)
            return carry

        lax.fori_loop(0, n_chip - 1, step, 0)
        send(partner, 1 - core)

    def send_init(other, c):
        to_slab(
            depth_send.at[c], depth_all.at[slab], init_send_sem.at[0], init_recv_sem.at[0], other
        ).start()
        to_slab(
            mw_send.at[c], mw_all.at[slab], init_send_sem.at[1], init_recv_sem.at[1], other
        ).start()

    def send_moments(k):
        def send(other, c):
            to_slab(
                moment_send.at[k, c],
                moment_all.at[k, slab],
                moment_send_sem.at[k],
                moment_recv_sem.at[k],
                other,
            ).start()

        each_slab(send)

    def others(ref, sem_send, sem_recv, count):
        return pltpu.make_async_remote_copy(
            src_ref=ref.at[pl.ds(0, count)],
            dst_ref=ref.at[pl.ds(0, count)],
            send_sem=sem_send,
            recv_sem=sem_recv,
            device_id={"slab": partner},
            device_id_type=pl.DeviceIdType.MESH,
        )

    each_slab(send_init)
    send_moments(0)

    others(depth_all, init_send_sem.at[0], init_recv_sem.at[0], n_slab - 1).wait_recv()
    depth_t[...] = depth_all[...].reshape(n_slab * 24, all_w).T
    depth_chip[0] = depth_all[slab].reshape(24, all_w)
    depth_chip[1] = depth_all[partner].reshape(24, all_w)
    others(mw_all, init_send_sem.at[1], init_recv_sem.at[1], n_slab - 1).wait_recv()

    view_order = sorted(
        [(dx, dy) for dx in range(n_xlo) for dy in range(n_y)],
        key=lambda p: -(p[0] + min(p[1], n_y - p[1])),
    )

    def view_of(step):
        dx, dy = step
        return lax.rem(x_lo + dx, n_xlo) * n_y + lax.rem(y + dy, n_y)

    def to_view(src, dst, send_sem, recv_sem, other):
        return pltpu.make_async_remote_copy(
            src_ref=src,
            dst_ref=dst,
            send_sem=send_sem,
            recv_sem=recv_sem,
            device_id={"view": other},
            device_id_type=pl.DeviceIdType.MESH,
        )

    for k in range(ITERS):
        if k > 0:
            send_moments(k)
        others(moment_all.at[k], moment_send_sem.at[k], moment_recv_sem.at[k], n_slab - 1).wait_recv()
        moments = moment_all[k].reshape(n_slab * 24, 128)
        projection = dot(depth_t[...], moments)
        seen = mw_all[:, 0].reshape(n_slab * rows_w, 128)
        weight = mw_all[:, 1].reshape(n_slab * rows_w, 128)
        residual = (weight * (seen - projection)).astype(BF16)
        spread_other = dot(depth_chip[1], residual).astype(BF16)
        for i in range(3):
            spread_send[k, i] = spread_other[8 * i : 8 * (i + 1)]
        hand = to_slab(
            spread_send.at[k], spread_recv.at[k], spread_send_sem.at[k], spread_recv_sem.at[k], partner
        )
        hand.start()
        spread_own = dot(depth_chip[0], residual)
        hand.wait_recv()

        def operands(spread):
            coarse = spread[0:16].astype(BF16)
            fine = spread[16:24].astype(BF16).astype(F32)
            fine = fine + pltpu.roll(fine, 4, 0)
            fine = jnp.concatenate([fine, fine], axis=0)
            return coarse, [(fine * m).astype(BF16) for m in masks]

        own_c, own_f = operands(spread_own)
        other_c, other_f = operands(spread_recv[k].astype(F32).reshape(24, 128))
        for step in view_order:
            b = view_of(step)
            base = b * width
            part = pl.ds(pl.multiple_of(base, 128), width)
            term_c = dot_nt(own_c, rays_c[core, part, :]) + dot_nt(other_c, rays_c[1 - core, part, :])
            term_f = jnp.zeros((16, 128), F32)
            for j in range(tiles):
                piece = pl.ds(pl.multiple_of(base + j * 128, 128), 128)
                term_f = term_f + dot_nt(own_f[j], rays_f[core, piece, :])
                term_f = term_f + dot_nt(other_f[j], rays_f[1 - core, piece, :])
            dest = back_recv.at[k, view] if step == (0, 0) else back_send.at[k, b]
            for j in range(tiles):
                dest[j] = term_c[:, j * 128 : (j + 1) * 128].astype(BF16)
            dest[tiles] = term_f.astype(BF16)
            if step != (0, 0):
                to_view(
                    back_send.at[k, b],
                    back_recv.at[k, view],
                    back_send_sem.at[k],
                    back_recv_sem.at[k, view],
                    b,
                ).start()
        total = back_recv[k, view].astype(F32)
        for step in reversed(view_order):
            if step == (0, 0):
                continue
            b = view_of(step)
            to_view(
                back_send.at[k, b], back_recv.at[k, b], back_send_sem.at[k], back_recv_sem.at[k, b], b
            ).wait_recv()
            total = total + back_recv[k, b].astype(F32)
        sum_send[k] = total.astype(BF16)
        for step in view_order:
            if step == (0, 0):
                continue
            to_view(
                sum_send.at[k],
                sum_recv.at[k, view],
                sum_send_sem.at[k],
                sum_recv_sem.at[k, view],
                view_of(step),
            ).start()
        acc = zero
        for step in reversed(view_order):
            b = view_of(step)
            if step == (0, 0):
                back = sum_send[k].astype(F32)
            else:
                to_view(
                    sum_send.at[k], sum_recv.at[k, b], sum_send_sem.at[k], sum_recv_sem.at[k, b], b
                ).wait_recv()
                back = sum_recv[k, b].astype(F32)
            for j in range(tiles):
                piece = pl.ds(pl.multiple_of(b * width + j * 128, 128), 128)
                vol_c[:, piece] = vol_c[:, piece] + wgt_c[:, piece] * back[j]
            vol_f[b] = vol_f[b] + wgt_f[b] * back[tiles]
            if k < ITERS - 1:
                acc = add_moment(b, acc)
        if k < ITERS - 1:
            finish_moment(k + 1, acc)

    coarse_out[...] = vol_c[...]
    for b in range(n_view):
        for j in range(tiles):
            part = slice(b * width + j * 128, b * width + (j + 1) * 128)
            fine_out[:, part] = vol_f[b, j * rows_f : (j + 1) * rows_f, :]

    others(depth_all, init_send_sem.at[0], init_recv_sem.at[0], n_slab - 1).wait_send()
    others(mw_all, init_send_sem.at[1], init_recv_sem.at[1], n_slab - 1).wait_send()
    for k in range(ITERS):
        others(
            moment_all.at[k], moment_send_sem.at[k], moment_recv_sem.at[k], n_slab - 1
        ).wait_send()
        to_slab(
            spread_send.at[k], spread_recv.at[k], spread_send_sem.at[k], spread_recv_sem.at[k], partner
        ).wait_send()
        others(back_send.at[k], back_send_sem.at[k], back_recv_sem.at[k, 0], n_view - 1).wait_send()
        others(back_send.at[k], sum_send_sem.at[k], back_recv_sem.at[k, 0], n_view - 1).wait_send()


def build(mesh, n_z, n_y):
    n_slab, n_view = mesh.shape["slab"], mesh.shape["view"]

    def body(*args):
        fine_volume, coarse_volume = args[0], args[1]
        rows_f, cells = fine_volume.shape
        rows_c = coarse_volume.shape[0]
        all_w = args[4].shape[2]
        rows_w = args[6].shape[0]
        width = cells // n_view
        tiles = width // 128
        anyspace = pl.BlockSpec(memory_space=pl.ANY)
        vmem = pl.BlockSpec(memory_space=pltpu.VMEM)
        smem = pl.BlockSpec(memory_space=pltpu.SMEM)
        dma = pltpu.SemaphoreType.DMA
        block = (tiles + 1, 16, 128)
        return pl.pallas_call(
            functools.partial(kernel, n_z, n_y, n_slab, n_view),
            name="sirt",
            out_shape=(
                jax.ShapeDtypeStruct((rows_f, cells), F32),
                jax.ShapeDtypeStruct((rows_c, cells), F32),
            ),
            in_specs=[anyspace] * 4 + [vmem] * 4 + [anyspace] * 2 + [smem] * 2,
            out_specs=(vmem, vmem),
            scratch_shapes=[
                pltpu.VMEM((2, cells, 128), BF16),
                pltpu.VMEM((2, cells, 128), BF16),
                pltpu.VMEM((2, rows_f, cells), F32),
                pltpu.VMEM((n_view, 16, 128), F32),
                pltpu.VMEM((n_view, 16, 128), F32),
                pltpu.VMEM((rows_c, cells), F32),
                pltpu.VMEM((rows_c, cells), F32),
                pltpu.VMEM((2, 3, 8, all_w), BF16),
                pltpu.VMEM((n_slab, 3, 8, all_w), BF16),
                pltpu.VMEM((all_w, n_slab * 24), BF16),
                pltpu.VMEM((2, 24, all_w), BF16),
                pltpu.VMEM((2, 2, rows_w, 128), F32),
                pltpu.VMEM((n_slab, 2, rows_w, 128), F32),
                pltpu.VMEM((ITERS, 2, 3, 8, 128), BF16),
                pltpu.VMEM((ITERS, n_slab, 3, 8, 128), BF16),
                pltpu.VMEM((ITERS, 3, 8, 128), BF16),
                pltpu.VMEM((ITERS, 3, 8, 128), BF16),
                pltpu.VMEM((ITERS, n_view) + block, BF16),
                pltpu.VMEM((ITERS, n_view) + block, BF16),
                pltpu.VMEM((ITERS,) + block, BF16),
                pltpu.VMEM((ITERS, n_view) + block, BF16),
                dma((4 + 2 * n_view,)),
                dma((2,)),
                dma((2,)),
                dma((ITERS,)),
                dma((ITERS,)),
                dma((ITERS,)),
                dma((ITERS,)),
                dma((ITERS,)),
                dma((ITERS, n_view)),
                dma((ITERS,)),
                dma((ITERS, n_view)),
            ],
            compiler_params=pltpu.CompilerParams(collective_id=0, has_side_effects=True),
        )(*args)

    return jax.shard_map(
        body,
        mesh=mesh,
        in_specs=(
            P("slab", None),
            P("slab", None),
            P("view", None, None),
            P("view", None, None),
            P("view", "slab", None),
            P("view", "slab", None),
            P("slab", "view", None),
            P("slab", "view", None),
            P("slab", None),
            P("slab", None),
            P("slab", None),
            P("view", "slab", None),
        ),
        out_specs=(P("slab", None), P("slab", None)),
        check_vma=False,
    )


def solution(mesh):
    return build(mesh, 8, 4)
```

time: 1110 us -> 87.8 us (0.08)
  waiting for transfers between devices: 890 us -> 0 us
  blocking collectives: 164 us -> 0 us
  Pallas kernels: 0 us -> 83.8 us
  matrix products: 24.1 us -> 0 us
  between operations: 14.4 us -> 0.64 us
    psum x6 -> x0, waiting for transfers between devices: 890 us -> none  [the longest x3 667 us: body(): lax.psum((total + jnp.einsum('vzw,vzu->wvu', coarse_depth, coarse_moment,...]
    all_gather x2 -> x0, blocking collectives: 84.1 us -> none  [the longest x1 46.7 us: body(): lax.all_gather(measured, 'slab', axis=0, tiled=True)]
    pallas_call x0 -> x1, Pallas kernels: none -> 83.8 us  [body(): pl.pallas_call(functools.partial(kernel, n_z, n_y, n_slab, n_view), name=...]
    psum x3 -> x0, blocking collectives: 80.3 us -> none  [body(): lax.psum(fine_term.astype(jnp.bfloat16), 'view').astype(jnp.float32)]
    dot_general x12 -> x0, matrix products: 24.1 us -> none  [the longest x3 7.09 us: body(): jnp.einsum('vzu,vxu->zx', fine_spread, fine_rays, preferred_element_type=...]
  transfers between devices with their start and end apart: 6 -> 0, of which waited for: 6 -> 0; matrix products, arithmetic and copies ran while one was open for 1% -> 0% of each run, Pallas kernels for 0% -> 0%
where the time goes in v1:
time: 87.8 us; the launch traced here: 87.6 us
  Pallas kernels  83.8 us (95%)
  local copies, waits for them, and re-layouts  3.14 us (4%)
    pallas_call x1, Pallas kernels, body(): pl.pallas_call(functools.partial(kernel, n_z, n_y, n_slab, n_view), name=...  83.8 us
    unnamed x2, local copies, waits for them, and re-layouts  3.14 us

profile of v1, /device:TPU:1, one launch (start us, length us, event | category | flops | bytes accessed | tf_op | source)
XLA Modules:
  0.0 87.6 jit_solution(13667789320299275887)
XLA Ops:
  0.6 83.8 %sirt.1 = (f32[4,4096]{1,0:T(4,128)}, f32[16,4096]{1,0:T(8,128)}) custom-call(f32[4,4096]{1,0:T(4,128)} %fine_volume.1, f32[16,4096]{1,0:T(8,128)} %coarse_volume.1, bf16[2,4096,128]{2,1,0:T(8,128)(2,1)} %fine_rays.1, bf16[2,4096,128]{2,1,0:T(8,128)(2,1)} %coarse_rays.1, bf16[2,4,256]{2,1,0:T(4,128)(2,1)} %fine_axial.1, bf16[2,16,256]{2,1,0:T(8,128)(2,1)} %coarse_axial.1, ...), custom_call_target="tpu_custom_call" | custom-call | tf_op jit(solution)/shard_map/sirt/pallas_call | solution.py:406
  84.5 1.5 %copy.16 = f32[4,4096]{1,0:T(4,128)} copy(f32[4,4096]{1,0:T(4,128)} %get-tuple-element.4) | data formatting | bytes 131072
  86.0 1.7 %copy.17 = f32[16,4096]{1,0:T(8,128)} copy(f32[16,4096]{1,0:T(8,128)} %get-tuple-element.5) | data formatting | bytes 524288

commit v2 on v1

--- a/solution.py
+++ b/solution.py
@@ -42,21 +42,28 @@
     coarse_out,
     rays_f,
     rays_c,
+    axial_f,
+    axial_c,
+    seen_in,
+    weight_in,
+    blocks,
+    hits,
     vol_in,
     vol_f,
     wgt_f,
     vol_c,
     wgt_c,
-    depth_send,
-    depth_all,
+    init_send,
+    init_all,
     depth_t,
     depth_chip,
-    mw_send,
-    mw_all,
+    seen,
+    weight,
     moment_send,
     moment_all,
     spread_send,
     spread_recv,
+    back_own,
     back_send,
     back_recv,
     sum_send,
@@ -91,9 +98,30 @@
     all_w = fine_axial.shape[2]
     n_tile = ray_hits.shape[2]
 
+    barrier = pltpu.get_barrier_semaphore()
+
+    def greet_slab(i, carry):
+        other = lax.rem(slab + 1 + i, n_slab)
+        pl.semaphore_signal(barrier, inc=1, device_id={"slab": other}, device_id_type=pl.DeviceIdType.MESH)
+        return carry
+
+    def greet_view(i, carry):
+        other = lax.rem(view + 1 + i, n_view)
+        pl.semaphore_signal(barrier, inc=1, device_id={"view": other}, device_id_type=pl.DeviceIdType.MESH)
+        return carry
+
+    lax.fori_loop(0, n_slab - 1, greet_slab, 0)
+    lax.fori_loop(0, n_view - 1, greet_view, 0)
+
     loads = []
     for i, (src, dst) in enumerate(
         [
+            (ray_hits, hits),
+            (fine_axial, axial_f),
+            (coarse_axial, axial_c),
+            (measured, seen_in),
+            (ray_weight, weight_in),
+            (margin_blocks, blocks),
             (coarse_volume, vol_c),
             (coarse_weight, wgt_c),
             (fine_volume, vol_in.at[0]),
@@ -109,49 +137,38 @@
         pair = []
         for i, (src, dst) in enumerate([(coarse_rays, rays_c), (fine_rays, rays_f)]):
             copy = pltpu.make_async_copy(
-                src.at[:, part, :], dst.at[:, part, :], load_sem.at[4 + 2 * b + i]
+                src.at[:, part, :], dst.at[:, part, :], load_sem.at[10 + 2 * b + i]
             )
             copy.start()
             pair.append(copy)
         ray_loads.append(pair)
 
-    barrier = pltpu.get_barrier_semaphore()
-
-    def greet_slab(i, carry):
-        other = lax.rem(slab + 1 + i, n_slab)
-        pl.semaphore_signal(barrier, inc=1, device_id={"slab": other}, device_id_type=pl.DeviceIdType.MESH)
-        return carry
-
-    def greet_view(i, carry):
-        other = lax.rem(view + 1 + i, n_view)
-        pl.semaphore_signal(barrier, inc=1, device_id={"view": other}, device_id_type=pl.DeviceIdType.MESH)
-        return carry
-
-    lax.fori_loop(0, n_slab - 1, greet_slab, 0)
-    lax.fori_loop(0, n_view - 1, greet_view, 0)
-
+    for copy in loads[:5]:
+        copy.wait()
+    half_w = all_w // 2
     row_tile = lax.broadcasted_iota(jnp.int32, (1, all_w), 1) // (all_w // n_tile)
     for v in range(2):
         hit = jnp.zeros((1, all_w), F32)
         for t in range(n_tile):
-            hit = jnp.where(row_tile == t, ray_hits[v, 0, t].astype(F32), hit)
-        dc = (coarse_axial[v].astype(F32) * hit).astype(BF16)
-        df = fine_axial[v].astype(F32) * hit
-        df = jnp.concatenate([df, jnp.zeros((8 - rows_f, all_w), F32)], axis=0)
-        depth_send[v, 0] = dc[0:8]
-        depth_send[v, 1] = dc[8:16]
-        depth_send[v, 2] = df.astype(BF16)
-        mw_send[v, 0] = measured[:, v, :]
-        mw_send[v, 1] = ray_weight[:, v, :]
-    depth_all[slab] = depth_send[core]
-    mw_all[slab] = mw_send[core]
-
-    for copy in loads:
+            hit = jnp.where(row_tile == t, hits[v, 0, t].astype(F32), hit)
+        dc = (axial_c[v].astype(F32) * hit).astype(BF16)
+        df = axial_f[v].astype(F32) * hit
+        df = jnp.concatenate([df[:, :half_w], df[:, half_w:]], axis=0)
+        init_send[v, 0] = dc[0:8, :half_w]
+        init_send[v, 1] = dc[8:16, :half_w]
+        init_send[v, 2] = dc[0:8, half_w:]
+        init_send[v, 3] = dc[8:16, half_w:]
+        init_send[v, 4] = df.astype(BF16)
+        init_send[v, 5] = seen_in[:, v, :].astype(BF16)
+        init_send[v, 6] = weight_in[:, v, :].astype(BF16)
+    init_all[slab] = init_send[core]
+
+    for copy in loads[5:]:
         copy.wait()
     block_id = lax.broadcasted_iota(jnp.int32, (1, cells), 1) // BLOCK
     keep = jnp.ones((1, cells), F32)
     for t in range(margin_blocks.shape[1]):
-        keep = jnp.where(block_id == margin_blocks[0, t], 0.0, keep)
+        keep = jnp.where(block_id == blocks[0, t], 0.0, keep)
     vol_c[...] = vol_c[...] * keep
     wgt_c[...] = wgt_c[...] * keep
     for b in range(n_view):
@@ -223,10 +240,7 @@
 
     def send_init(other, c):
         to_slab(
-            depth_send.at[c], depth_all.at[slab], init_send_sem.at[0], init_recv_sem.at[0], other
-        ).start()
-        to_slab(
-            mw_send.at[c], mw_all.at[slab], init_send_sem.at[1], init_recv_sem.at[1], other
+            init_send.at[c], init_all.at[slab], init_send_sem.at[0], init_recv_sem.at[0], other
         ).start()
 
     def send_moments(k):
@@ -254,11 +268,24 @@
     each_slab(send_init)
     send_moments(0)
 
-    others(depth_all, init_send_sem.at[0], init_recv_sem.at[0], n_slab - 1).wait_recv()
-    depth_t[...] = depth_all[...].reshape(n_slab * 24, all_w).T
-    depth_chip[0] = depth_all[slab].reshape(24, all_w)
-    depth_chip[1] = depth_all[partner].reshape(24, all_w)
-    others(mw_all, init_send_sem.at[1], init_recv_sem.at[1], n_slab - 1).wait_recv()
+    others(init_all, init_send_sem.at[0], init_recv_sem.at[0], n_slab - 1).wait_recv()
+    upper = lax.broadcasted_iota(jnp.int32, (8, 128), 0) >= rows_f
+    for h in range(2):
+        cols = slice(h * half_w, (h + 1) * half_w)
+        fine = init_all[:, 4].astype(F32)
+        fine = jnp.where(upper if h else jnp.logical_not(upper), fine, 0.0).astype(BF16)
+        depth = jnp.concatenate(
+            [init_all[:, 2 * h], init_all[:, 2 * h + 1], fine], axis=1
+        ).reshape(n_slab * 24, half_w)
+        depth_t[cols, :] = depth.T
+        for i, index in enumerate((slab, partner)):
+            own = init_all[index, 4].astype(F32)
+            own = jnp.where(upper if h else jnp.logical_not(upper), own, 0.0).astype(BF16)
+            depth_chip[i, 0:8, cols] = init_all[index, 2 * h]
+            depth_chip[i, 8:16, cols] = init_all[index, 2 * h + 1]
+            depth_chip[i, 16:24, cols] = own
+    seen[...] = init_all[:, 5].astype(F32).reshape(n_slab * rows_w, 128)
+    weight[...] = init_all[:, 6].astype(F32).reshape(n_slab * rows_w, 128)
 
     view_order = sorted(
         [(dx, dy) for dx in range(n_xlo) for dy in range(n_y)],
@@ -285,38 +312,49 @@
         others(moment_all.at[k], moment_send_sem.at[k], moment_recv_sem.at[k], n_slab - 1).wait_recv()
         moments = moment_all[k].reshape(n_slab * 24, 128)
         projection = dot(depth_t[...], moments)
-        seen = mw_all[:, 0].reshape(n_slab * rows_w, 128)
-        weight = mw_all[:, 1].reshape(n_slab * rows_w, 128)
-        residual = (weight * (seen - projection)).astype(BF16)
-        spread_other = dot(depth_chip[1], residual).astype(BF16)
+        residual = (weight[...] * (seen[...] - projection)).astype(BF16)
+
+        def spread_of(depth):
+            spread = dot(depth, residual)
+            fine = spread[16:24]
+            return jnp.concatenate([spread[0:16], fine + pltpu.roll(fine, 4, 0)], axis=0).astype(BF16)
+
+        spread_other = spread_of(depth_chip[1])
         for i in range(3):
             spread_send[k, i] = spread_other[8 * i : 8 * (i + 1)]
         hand = to_slab(
             spread_send.at[k], spread_recv.at[k], spread_send_sem.at[k], spread_recv_sem.at[k], partner
         )
         hand.start()
-        spread_own = dot(depth_chip[0], residual)
-        hand.wait_recv()
+        spread_own = spread_of(depth_chip[0])
 
         def operands(spread):
-            coarse = spread[0:16].astype(BF16)
-            fine = spread[16:24].astype(BF16).astype(F32)
-            fine = fine + pltpu.roll(fine, 4, 0)
+            fine = spread[16:24].astype(F32)
             fine = jnp.concatenate([fine, fine], axis=0)
-            return coarse, [(fine * m).astype(BF16) for m in masks]
-
-        own_c, own_f = operands(spread_own)
-        other_c, other_f = operands(spread_recv[k].astype(F32).reshape(24, 128))
-        for step in view_order:
-            b = view_of(step)
+            return spread[0:16], [(fine * m).astype(BF16) for m in masks]
+
+        def terms(coarse, fine, v, b):
             base = b * width
             part = pl.ds(pl.multiple_of(base, 128), width)
-            term_c = dot_nt(own_c, rays_c[core, part, :]) + dot_nt(other_c, rays_c[1 - core, part, :])
+            term_c = dot_nt(coarse, rays_c[v, part, :])
             term_f = jnp.zeros((16, 128), F32)
             for j in range(tiles):
                 piece = pl.ds(pl.multiple_of(base + j * 128, 128), 128)
-                term_f = term_f + dot_nt(own_f[j], rays_f[core, piece, :])
-                term_f = term_f + dot_nt(other_f[j], rays_f[1 - core, piece, :])
+                term_f = term_f + dot_nt(fine[j], rays_f[v, piece, :])
+            return term_c, term_f
+
+        own_c, own_f = operands(spread_own)
+        for i, step in enumerate(view_order):
+            term_c, term_f = terms(own_c, own_f, core, view_of(step))
+            back_own[i, :, 0:width] = term_c
+            back_own[i, :, width : width + 128] = term_f
+        hand.wait_recv()
+        other_c, other_f = operands(spread_recv[k].reshape(24, 128))
+        for i, step in enumerate(view_order):
+            b = view_of(step)
+            term_c, term_f = terms(other_c, other_f, 1 - core, b)
+            term_c = term_c + back_own[i, :, 0:width]
+            term_f = term_f + back_own[i, :, width : width + 128]
             dest = back_recv.at[k, view] if step == (0, 0) else back_send.at[k, b]
             for j in range(tiles):
                 dest[j] = term_c[:, j * 128 : (j + 1) * 128].astype(BF16)
@@ -374,8 +412,7 @@
             part = slice(b * width + j * 128, b * width + (j + 1) * 128)
             fine_out[:, part] = vol_f[b, j * rows_f : (j + 1) * rows_f, :]
 
-    others(depth_all, init_send_sem.at[0], init_recv_sem.at[0], n_slab - 1).wait_send()
-    others(mw_all, init_send_sem.at[1], init_recv_sem.at[1], n_slab - 1).wait_send()
+    others(init_all, init_send_sem.at[0], init_recv_sem.at[0], n_slab - 1).wait_send()
     for k in range(ITERS):
         others(
             moment_all.at[k], moment_send_sem.at[k], moment_recv_sem.at[k], n_slab - 1
@@ -385,6 +422,17 @@
         ).wait_send()
         others(back_send.at[k], back_send_sem.at[k], back_recv_sem.at[k, 0], n_view - 1).wait_send()
         others(back_send.at[k], sum_send_sem.at[k], back_recv_sem.at[k, 0], n_view - 1).wait_send()
+
+
+def put_out(fine, coarse, fine_out, coarse_out, sem):
+    copies = [
+        pltpu.make_async_copy(src, dst, sem.at[i])
+        for i, (src, dst) in enumerate([(coarse, coarse_out), (fine, fine_out)])
+    ]
+    for copy in copies:
+        copy.start()
+    for copy in copies:
+        copy.wait()
 
 
 def build(mesh, n_z, n_y):
@@ -400,43 +448,47 @@
         tiles = width // 128
         anyspace = pl.BlockSpec(memory_space=pl.ANY)
         vmem = pl.BlockSpec(memory_space=pltpu.VMEM)
-        smem = pl.BlockSpec(memory_space=pltpu.SMEM)
         dma = pltpu.SemaphoreType.DMA
         block = (tiles + 1, 16, 128)
-        return pl.pallas_call(
+        shapes = ((rows_f, cells), (rows_c, cells))
+        results = pl.pallas_call(
             functools.partial(kernel, n_z, n_y, n_slab, n_view),
             name="sirt",
-            out_shape=(
-                jax.ShapeDtypeStruct((rows_f, cells), F32),
-                jax.ShapeDtypeStruct((rows_c, cells), F32),
-            ),
-            in_specs=[anyspace] * 4 + [vmem] * 4 + [anyspace] * 2 + [smem] * 2,
+            out_shape=tuple(pltpu.VMEM(shape, F32) for shape in shapes),
+            in_specs=[anyspace] * 12,
             out_specs=(vmem, vmem),
             scratch_shapes=[
                 pltpu.VMEM((2, cells, 128), BF16),
                 pltpu.VMEM((2, cells, 128), BF16),
+                pltpu.VMEM(args[4].shape, BF16),
+                pltpu.VMEM(args[5].shape, BF16),
+                pltpu.VMEM(args[6].shape, F32),
+                pltpu.VMEM(args[7].shape, F32),
+                pltpu.SMEM(args[10].shape, jnp.int32),
+                pltpu.SMEM(args[11].shape, jnp.int32),
                 pltpu.VMEM((2, rows_f, cells), F32),
                 pltpu.VMEM((n_view, 16, 128), F32),
                 pltpu.VMEM((n_view, 16, 128), F32),
                 pltpu.VMEM((rows_c, cells), F32),
                 pltpu.VMEM((rows_c, cells), F32),
-                pltpu.VMEM((2, 3, 8, all_w), BF16),
-                pltpu.VMEM((n_slab, 3, 8, all_w), BF16),
+                pltpu.VMEM((2, 7, 8, 128), BF16),
+                pltpu.VMEM((n_slab, 7, 8, 128), BF16),
                 pltpu.VMEM((all_w, n_slab * 24), BF16),
                 pltpu.VMEM((2, 24, all_w), BF16),
-                pltpu.VMEM((2, 2, rows_w, 128), F32),
-                pltpu.VMEM((n_slab, 2, rows_w, 128), F32),
+                pltpu.VMEM((n_slab * rows_w, 128), F32),
+                pltpu.VMEM((n_slab * rows_w, 128), F32),
                 pltpu.VMEM((ITERS, 2, 3, 8, 128), BF16),
                 pltpu.VMEM((ITERS, n_slab, 3, 8, 128), BF16),
                 pltpu.VMEM((ITERS, 3, 8, 128), BF16),
                 pltpu.VMEM((ITERS, 3, 8, 128), BF16),
+                pltpu.VMEM((n_view, 16, width + 128), F32),
                 pltpu.VMEM((ITERS, n_view) + block, BF16),
                 pltpu.VMEM((ITERS, n_view) + block, BF16),
                 pltpu.VMEM((ITERS,) + block, BF16),
                 pltpu.VMEM((ITERS, n_view) + block, BF16),
-                dma((4 + 2 * n_view,)),
-                dma((2,)),
-                dma((2,)),
+                dma((10 + 2 * n_view,)),
+                dma((1,)),
+                dma((1,)),
                 dma((ITERS,)),
                 dma((ITERS,)),
                 dma((ITERS,)),
@@ -448,6 +500,14 @@
             ],
             compiler_params=pltpu.CompilerParams(collective_id=0, has_side_effects=True),
         )(*args)
+        return pl.pallas_call(
+            put_out,
+            name="put_out",
+            out_shape=tuple(jax.ShapeDtypeStruct(shape, F32) for shape in shapes),
+            in_specs=[vmem, vmem],
+            out_specs=(anyspace, anyspace),
+            scratch_shapes=[dma((2,))],
+        )(*(pltpu.with_memory_space_constraint(r, pltpu.VMEM) for r in results))
 
     return jax.shard_map(
         body,

time: 87.8 us -> 77.4 us (0.88)
  Pallas kernels: 83.8 us -> 76.7 us
  local copies, waits for them, and re-layouts: 3.14 us -> 0 us
    pallas_call x1, Pallas kernels: 83.8 us -> 76 us  [body(): pl.pallas_call(functools.partial(kernel, n_z, n_y, n_slab, n_view), name=...]
    unnamed x2 -> x0, local copies, waits for them, and re-layouts: 3.14 us -> none
where the time goes in v2:
time: 77.4 us
  Pallas kernels  76.7 us (99%)
    pallas_call x1, Pallas kernels, body(): pl.pallas_call(functools.partial(kernel, n_z, n_y, n_slab, n_view), name=...  76 us

profile of v2, /device:TPU:1, one launch (start us, length us, event | category | flops | bytes accessed | tf_op | source)
XLA Modules:
  0.0 77.4 jit_solution(8652214041197415064)
XLA Ops:
  0.6 76.0 %sirt.1 = (f32[4,4096]{1,0:T(4,128)S(1)}, f32[16,4096]{1,0:T(8,128)S(1)}) custom-call(f32[4,4096]{1,0:T(4,128)} %fine_volume.1, f32[16,4096]{1,0:T(8,128)} %coarse_volume.1, bf16[2,4096,128]{2,1,0:T(8,128)(2,1)} %fine_rays.1, bf16[2,4096,128]{2,1,0:T(8,128)(2,1)} %coarse_rays.1, bf16[2,4,256]{2,1,0:T(4,128)(2,1)} %fine_axial.1, ...), custom_call_target="tpu_custom_call" | custom-call | tf_op jit(solution)/shard_map/sirt/pallas_call | solution.py:454
  76.6 0.7 put_out.1

commit v3 on v2

--- a/solution.py
+++ b/solution.py
@@ -57,6 +57,11 @@
     init_all,
     depth_t,
     depth_chip,
+    depth_own,
+    part_send,
+    part_recv,
+    rest_send,
+    rest_recv,
     seen,
     weight,
     moment_send,
@@ -71,6 +76,8 @@
     load_sem,
     init_send_sem,
     init_recv_sem,
+    first_send_sem,
+    first_recv_sem,
     moment_send_sem,
     moment_recv_sem,
     spread_send_sem,
@@ -163,6 +170,28 @@
         init_send[v, 6] = weight_in[:, v, :].astype(BF16)
     init_all[slab] = init_send[core]
 
+    upper = lax.broadcasted_iota(jnp.int32, (8, 128), 0) >= rows_f
+
+    def fine_half(packed, h):
+        mine = upper if h else jnp.logical_not(upper)
+        return jnp.where(mine, packed.astype(F32), 0.0).astype(BF16)
+
+    for v in range(2):
+        for h in range(2):
+            depth = jnp.concatenate(
+                [init_send[v, 2 * h], init_send[v, 2 * h + 1], fine_half(init_send[v, 4], h)], axis=0
+            )
+            depth_own[v, h * half_w : (h + 1) * half_w, :] = depth.T
+
+    def chip_depth(i, index):
+        for h in range(2):
+            cols = slice(h * half_w, (h + 1) * half_w)
+            depth_chip[i, 0:8, cols] = init_all[index, 2 * h]
+            depth_chip[i, 8:16, cols] = init_all[index, 2 * h + 1]
+            depth_chip[i, 16:24, cols] = fine_half(init_all[index, 4], h)
+
+    chip_depth(0, slab)
+
     for copy in loads[5:]:
         copy.wait()
     block_id = lax.broadcasted_iota(jnp.int32, (1, cells), 1) // BLOCK
@@ -200,7 +229,8 @@
             moment_send[k, v, 0] = mc[0:8]
             moment_send[k, v, 1] = mc[8:16]
             moment_send[k, v, 2] = whole.astype(BF16)
-        moment_all[k, slab] = moment_send[k, core]
+        if k > 0:
+            moment_all[k, slab] = moment_send[k, core]
 
     zero = [jnp.zeros((16, 128), F32) for _ in range(4)]
     acc = zero
@@ -209,6 +239,11 @@
             copy.wait()
         acc = add_moment(b, acc)
     finish_moment(0, acc)
+    for v in range(2):
+        part = dot(depth_own[v], moment_send[0, v].reshape(24, 128)).astype(BF16)
+        for i in range(n_slab):
+            part_send[i, v] = part[i * rows_w : (i + 1) * rows_w]
+    part_recv[slab] = part_send[slab]
 
     pl.semaphore_wait(barrier, n_slab + n_view - 2)
 
@@ -224,7 +259,7 @@
 
     n_chip = n_xhi * n_z
 
-    def each_slab(send):
+    def each_slab(send, first=0, last=n_chip - 1):
         def step(i, carry):
             turn = lax.rem(i, n_z)
             half = (turn + 1) // 2
@@ -235,8 +270,7 @@
                 send(2 * chip + c, c)
             return carry
 
-        lax.fori_loop(0, n_chip - 1, step, 0)
-        send(partner, 1 - core)
+        lax.fori_loop(first, last, step, 0)
 
     def send_init(other, c):
         to_slab(
@@ -254,6 +288,7 @@
             ).start()
 
         each_slab(send)
+        send(partner, 1 - core)
 
     def others(ref, sem_send, sem_recv, count):
         return pltpu.make_async_remote_copy(
@@ -265,27 +300,45 @@
             device_id_type=pl.DeviceIdType.MESH,
         )
 
-    each_slab(send_init)
-    send_moments(0)
-
-    others(init_all, init_send_sem.at[0], init_recv_sem.at[0], n_slab - 1).wait_recv()
-    upper = lax.broadcasted_iota(jnp.int32, (8, 128), 0) >= rows_f
-    for h in range(2):
-        cols = slice(h * half_w, (h + 1) * half_w)
-        fine = init_all[:, 4].astype(F32)
-        fine = jnp.where(upper if h else jnp.logical_not(upper), fine, 0.0).astype(BF16)
-        depth = jnp.concatenate(
-            [init_all[:, 2 * h], init_all[:, 2 * h + 1], fine], axis=1
-        ).reshape(n_slab * 24, half_w)
-        depth_t[cols, :] = depth.T
-        for i, index in enumerate((slab, partner)):
-            own = init_all[index, 4].astype(F32)
-            own = jnp.where(upper if h else jnp.logical_not(upper), own, 0.0).astype(BF16)
-            depth_chip[i, 0:8, cols] = init_all[index, 2 * h]
-            depth_chip[i, 8:16, cols] = init_all[index, 2 * h + 1]
-            depth_chip[i, 16:24, cols] = own
-    seen[...] = init_all[:, 5].astype(F32).reshape(n_slab * rows_w, 128)
-    weight[...] = init_all[:, 6].astype(F32).reshape(n_slab * rows_w, 128)
+    def send_part(other, c):
+        to_slab(
+            part_send.at[other],
+            part_recv.at[slab],
+            first_send_sem.at[0],
+            first_recv_sem.at[0],
+            other,
+        ).start()
+
+    def send_rest(other, c):
+        to_slab(
+            rest_send.at[c], rest_recv.at[slab], first_send_sem.at[1], first_recv_sem.at[1], other
+        ).start()
+
+    each_slab(send_part)
+    send_part(partner, 1 - core)
+    init_hand = to_slab(
+        init_send.at[1 - core], init_all.at[slab], init_send_sem.at[1], init_recv_sem.at[1], partner
+    )
+    init_hand.start()
+    init_hand.wait_recv()
+    chip_depth(1, partner)
+    others(part_recv, first_send_sem.at[0], first_recv_sem.at[0], n_slab - 1).wait_recv()
+    summed = jnp.sum(part_recv[...].astype(F32), axis=0)
+    for v in range(2):
+        rest_send[v] = (weight_in[:, v, :] * (seen_in[:, v, :] - summed[v])).astype(BF16)
+    rest_recv[slab] = rest_send[core]
+    each_slab(send_rest)
+    send_rest(partner, 1 - core)
+
+    def finish_init():
+        others(init_all, init_send_sem.at[0], init_recv_sem.at[0], n_slab - 2).wait_recv()
+        for h in range(2):
+            depth = jnp.concatenate(
+                [init_all[:, 2 * h], init_all[:, 2 * h + 1], fine_half(init_all[:, 4], h)], axis=1
+            )
+            depth_t[h * half_w : (h + 1) * half_w, :] = depth.reshape(n_slab * 24, half_w).T
+        seen[...] = init_all[:, 5].astype(F32).reshape(n_slab * rows_w, 128)
+        weight[...] = init_all[:, 6].astype(F32).reshape(n_slab * rows_w, 128)
 
     view_order = sorted(
         [(dx, dy) for dx in range(n_xlo) for dy in range(n_y)],
@@ -307,26 +360,34 @@
         )
 
     for k in range(ITERS):
-        if k > 0:
+        if k == 0:
+            others(rest_recv, first_send_sem.at[1], first_recv_sem.at[1], n_slab - 1).wait_recv()
+            residual = rest_recv[...].reshape(n_slab * rows_w, 128)
+            each_slab(send_init, n_chip - n_z, n_chip - 1)
+        else:
             send_moments(k)
-        others(moment_all.at[k], moment_send_sem.at[k], moment_recv_sem.at[k], n_slab - 1).wait_recv()
-        moments = moment_all[k].reshape(n_slab * 24, 128)
-        projection = dot(depth_t[...], moments)
-        residual = (weight[...] * (seen[...] - projection)).astype(BF16)
-
-        def spread_of(depth):
-            spread = dot(depth, residual)
+            if k == 1:
+                finish_init()
+            others(
+                moment_all.at[k], moment_send_sem.at[k], moment_recv_sem.at[k], n_slab - 1
+            ).wait_recv()
+            projection = dot(depth_t[...], moment_all[k].reshape(n_slab * 24, 128))
+            residual = (weight[...] * (seen[...] - projection)).astype(BF16)
+
+        both = dot(depth_chip[...].reshape(48, all_w), residual)
+
+        def spread_of(spread):
             fine = spread[16:24]
             return jnp.concatenate([spread[0:16], fine + pltpu.roll(fine, 4, 0)], axis=0).astype(BF16)
 
-        spread_other = spread_of(depth_chip[1])
+        spread_other = spread_of(both[24:48])
         for i in range(3):
             spread_send[k, i] = spread_other[8 * i : 8 * (i + 1)]
         hand = to_slab(
             spread_send.at[k], spread_recv.at[k], spread_send_sem.at[k], spread_recv_sem.at[k], partner
         )
         hand.start()
-        spread_own = spread_of(depth_chip[0])
+        spread_own = spread_of(both[0:24])
 
         def operands(spread):
             fine = spread[16:24].astype(F32)
@@ -367,6 +428,8 @@
                     back_recv_sem.at[k, view],
                     b,
                 ).start()
+        if k == 0:
+            each_slab(send_init, 0, n_chip - n_z)
         total = back_recv[k, view].astype(F32)
         for step in reversed(view_order):
             if step == (0, 0):
@@ -412,11 +475,15 @@
             part = slice(b * width + j * 128, b * width + (j + 1) * 128)
             fine_out[:, part] = vol_f[b, j * rows_f : (j + 1) * rows_f, :]
 
-    others(init_all, init_send_sem.at[0], init_recv_sem.at[0], n_slab - 1).wait_send()
+    others(init_all, init_send_sem.at[0], init_recv_sem.at[0], n_slab - 2).wait_send()
+    init_hand.wait_send()
+    others(part_recv, first_send_sem.at[0], first_recv_sem.at[0], n_slab - 1).wait_send()
+    others(rest_recv, first_send_sem.at[1], first_recv_sem.at[1], n_slab - 1).wait_send()
     for k in range(ITERS):
-        others(
-            moment_all.at[k], moment_send_sem.at[k], moment_recv_sem.at[k], n_slab - 1
-        ).wait_send()
+        if k > 0:
+            others(
+                moment_all.at[k], moment_send_sem.at[k], moment_recv_sem.at[k], n_slab - 1
+            ).wait_send()
         to_slab(
             spread_send.at[k], spread_recv.at[k], spread_send_sem.at[k], spread_recv_sem.at[k], partner
         ).wait_send()
@@ -475,6 +542,11 @@
                 pltpu.VMEM((n_slab, 7, 8, 128), BF16),
                 pltpu.VMEM((all_w, n_slab * 24), BF16),
                 pltpu.VMEM((2, 24, all_w), BF16),
+                pltpu.VMEM((2, all_w, 24), BF16),
+                pltpu.VMEM((n_slab, 2, rows_w, 128), BF16),
+                pltpu.VMEM((n_slab, 2, rows_w, 128), BF16),
+                pltpu.VMEM((2, rows_w, 128), BF16),
+                pltpu.VMEM((n_slab, rows_w, 128), BF16),
                 pltpu.VMEM((n_slab * rows_w, 128), F32),
                 pltpu.VMEM((n_slab * rows_w, 128), F32),
                 pltpu.VMEM((ITERS, 2, 3, 8, 128), BF16),
@@ -487,8 +559,10 @@
                 pltpu.VMEM((ITERS,) + block, BF16),
                 pltpu.VMEM((ITERS, n_view) + block, BF16),
                 dma((10 + 2 * n_view,)),
-                dma((1,)),
-                dma((1,)),
+                dma((2,)),
+                dma((2,)),
+                dma((2,)),
+                dma((2,)),
                 dma((ITERS,)),
                 dma((ITERS,)),
                 dma((ITERS,)),

time: 77.4 us -> 76.7 us (level)
  Pallas kernels: 76.7 us -> 75.9 us
where the time goes in v3:
time: 76.7 us; the launch traced here: 76.6 us
  Pallas kernels  75.9 us (99%)
    pallas_call x1, Pallas kernels, body(): pl.pallas_call(functools.partial(kernel, n_z, n_y, n_slab, n_view), name=...  75.2 us

profile of v3, /device:TPU:1, one launch (start us, length us, event | category | flops | bytes accessed | tf_op | source)
XLA Modules:
  0.0 76.6 jit_solution(6857016061994848850)
XLA Ops:
  0.6 75.2 %sirt.1 = (f32[4,4096]{1,0:T(4,128)S(1)}, f32[16,4096]{1,0:T(8,128)S(1)}) custom-call(f32[4,4096]{1,0:T(4,128)} %fine_volume.1, f32[16,4096]{1,0:T(8,128)} %coarse_volume.1, bf16[2,4096,128]{2,1,0:T(8,128)(2,1)} %fine_rays.1, bf16[2,4096,128]{2,1,0:T(8,128)(2,1)} %coarse_rays.1, bf16[2,4,256]{2,1,0:T(4,128)(2,1)} %fine_axial.1, ...), custom_call_target="tpu_custom_call" | custom-call | tf_op jit(solution)/shard_map/sirt/pallas_call | solution.py:521
  75.8 0.7 put_out.1

commit v4 on v3

--- a/solution.py
+++ b/solution.py
@@ -329,6 +329,7 @@
     rest_recv[slab] = rest_send[core]
     each_slab(send_rest)
     send_rest(partner, 1 - core)
+    each_slab(send_init, 0, n_chip - n_z)
 
     def finish_init():
         others(init_all, init_send_sem.at[0], init_recv_sem.at[0], n_slab - 2).wait_recv()
@@ -363,7 +364,6 @@
         if k == 0:
             others(rest_recv, first_send_sem.at[1], first_recv_sem.at[1], n_slab - 1).wait_recv()
             residual = rest_recv[...].reshape(n_slab * rows_w, 128)
-            each_slab(send_init, n_chip - n_z, n_chip - 1)
         else:
             send_moments(k)
             if k == 1:
@@ -387,6 +387,8 @@
             spread_send.at[k], spread_recv.at[k], spread_send_sem.at[k], spread_recv_sem.at[k], partner
         )
         hand.start()
+        if k == 0:
+            each_slab(send_init, n_chip - n_z, n_chip - 1)
         spread_own = spread_of(both[0:24])
 
         def operands(spread):
@@ -428,8 +430,6 @@
                     back_recv_sem.at[k, view],
                     b,
                 ).start()
-        if k == 0:
-            each_slab(send_init, 0, n_chip - n_z)
         total = back_recv[k, view].astype(F32)
         for step in reversed(view_order):
             if step == (0, 0):

time: 76.7 us -> 73.2 us (0.954)
  Pallas kernels: 75.9 us -> 72.5 us
    pallas_call x1, Pallas kernels: 75.2 us -> 71.8 us  [body(): pl.pallas_call(functools.partial(kernel, n_z, n_y, n_slab, n_view), name=...]
where the time goes in v4:
time: 73.2 us; the launch traced here: 73.1 us
  Pallas kernels  72.5 us (99%)
    pallas_call x1, Pallas kernels, body(): pl.pallas_call(functools.partial(kernel, n_z, n_y, n_slab, n_view), name=...  71.8 us

profile of v4, /device:TPU:1, one launch (start us, length us, event | category | flops | bytes accessed | tf_op | source)
XLA Modules:
  0.0 73.1 jit_solution(3332745522846936417)
XLA Ops:
  0.6 71.8 %sirt.1 = (f32[4,4096]{1,0:T(4,128)S(1)}, f32[16,4096]{1,0:T(8,128)S(1)}) custom-call(f32[4,4096]{1,0:T(4,128)} %fine_volume.1, f32[16,4096]{1,0:T(8,128)} %coarse_volume.1, bf16[2,4096,128]{2,1,0:T(8,128)(2,1)} %fine_rays.1, bf16[2,4096,128]{2,1,0:T(8,128)(2,1)} %coarse_rays.1, bf16[2,4,256]{2,1,0:T(4,128)(2,1)} %fine_axial.1, ...), custom_call_target="tpu_custom_call" | custom-call | tf_op jit(solution)/shard_map/sirt/pallas_call | solution.py:521
  72.4 0.7 %put_out.1 = (f32[4,4096]{1,0:T(4,128)}, f32[16,4096]{1,0:T(8,128)}) custom-call(f32[4,4096]{1,0:T(4,128)S(1)} %get-tuple-element.4.fine, f32[16,4096]{1,0:T(8,128)S(1)} %get-tuple-element.5.coarse), custom_call_target="tpu_custom_call" | custom-call | tf_op jit(solution)/shard_map/put_out/pallas_call | solution.py:577

commit v5 on v4

--- a/solution.py
+++ b/solution.py
@@ -51,7 +51,6 @@
     vol_in,
     vol_f,
     wgt_f,
-    vol_c,
     wgt_c,
     init_send,
     init_all,
@@ -97,6 +96,7 @@
     x_lo = view // n_y
     n_xlo = n_view // n_y
     partner = slab + 1 - 2 * core
+    vol_c = coarse_out
     cells = coarse_volume.shape[1]
     width = cells // n_view
     tiles = width // 128
@@ -107,17 +107,26 @@
 
     barrier = pltpu.get_barrier_semaphore()
 
-    def greet_slab(i, carry):
-        other = lax.rem(slab + 1 + i, n_slab)
+    along_z = sorted(range(n_z), key=lambda dz: -min(dz, n_z - dz))
+    far_chips = [(dx, dz) for dx in range(n_xhi - 1, 0, -1) for dz in along_z]
+    near_chips = [(0, dz) for dz in along_z if dz]
+
+    def each_slab(send, chips=far_chips + near_chips):
+        for dx, dz in chips:
+            chip = lax.rem(x_hi + dx, n_xhi) * n_z + lax.rem(z + dz, n_z)
+            for c in range(2):
+                send(2 * chip + c, c, dx)
+
+    def greet(other, c, dx):
         pl.semaphore_signal(barrier, inc=1, device_id={"slab": other}, device_id_type=pl.DeviceIdType.MESH)
-        return carry
 
     def greet_view(i, carry):
         other = lax.rem(view + 1 + i, n_view)
         pl.semaphore_signal(barrier, inc=1, device_id={"view": other}, device_id_type=pl.DeviceIdType.MESH)
         return carry
 
-    lax.fori_loop(0, n_slab - 1, greet_slab, 0)
+    each_slab(greet)
+    greet(partner, 1 - core, 0)
     lax.fori_loop(0, n_view - 1, greet_view, 0)
 
     loads = []
@@ -257,38 +266,23 @@
             device_id_type=pl.DeviceIdType.MESH,
         )
 
-    n_chip = n_xhi * n_z
-
-    def each_slab(send, first=0, last=n_chip - 1):
-        def step(i, carry):
-            turn = lax.rem(i, n_z)
-            half = (turn + 1) // 2
-            dz = n_z // 2 + half * (2 * lax.rem(turn, 2) - 1)
-            dx = n_xhi - 1 - i // n_z
-            chip = lax.rem(x_hi + dx, n_xhi) * n_z + lax.rem(z + dz + n_z, n_z)
-            for c in range(2):
-                send(2 * chip + c, c)
-            return carry
-
-        lax.fori_loop(first, last, step, 0)
-
-    def send_init(other, c):
+    def send_init(other, c, dx):
         to_slab(
             init_send.at[c], init_all.at[slab], init_send_sem.at[0], init_recv_sem.at[0], other
         ).start()
 
     def send_moments(k):
-        def send(other, c):
+        def send(other, c, dx):
             to_slab(
                 moment_send.at[k, c],
                 moment_all.at[k, slab],
                 moment_send_sem.at[k],
-                moment_recv_sem.at[k],
+                moment_recv_sem.at[k, 0],
                 other,
             ).start()
 
         each_slab(send)
-        send(partner, 1 - core)
+        send(partner, 1 - core, 0)
 
     def others(ref, sem_send, sem_recv, count):
         return pltpu.make_async_remote_copy(
@@ -300,7 +294,7 @@
             device_id_type=pl.DeviceIdType.MESH,
         )
 
-    def send_part(other, c):
+    def send_part(other, c, dx):
         to_slab(
             part_send.at[other],
             part_recv.at[slab],
@@ -309,13 +303,13 @@
             other,
         ).start()
 
-    def send_rest(other, c):
+    def send_rest(other, c, dx):
         to_slab(
             rest_send.at[c], rest_recv.at[slab], first_send_sem.at[1], first_recv_sem.at[1], other
         ).start()
 
     each_slab(send_part)
-    send_part(partner, 1 - core)
+    send_part(partner, 1 - core, 0)
     init_hand = to_slab(
         init_send.at[1 - core], init_all.at[slab], init_send_sem.at[1], init_recv_sem.at[1], partner
     )
@@ -328,8 +322,8 @@
         rest_send[v] = (weight_in[:, v, :] * (seen_in[:, v, :] - summed[v])).astype(BF16)
     rest_recv[slab] = rest_send[core]
     each_slab(send_rest)
-    send_rest(partner, 1 - core)
-    each_slab(send_init, 0, n_chip - n_z)
+    send_rest(partner, 1 - core, 0)
+    each_slab(send_init, far_chips)
 
     def finish_init():
         others(init_all, init_send_sem.at[0], init_recv_sem.at[0], n_slab - 2).wait_recv()
@@ -369,7 +363,7 @@
             if k == 1:
                 finish_init()
             others(
-                moment_all.at[k], moment_send_sem.at[k], moment_recv_sem.at[k], n_slab - 1
+                moment_all.at[k], moment_send_sem.at[k], moment_recv_sem.at[k, 0], n_slab - 1
             ).wait_recv()
             projection = dot(depth_t[...], moment_all[k].reshape(n_slab * 24, 128))
             residual = (weight[...] * (seen[...] - projection)).astype(BF16)
@@ -388,7 +382,7 @@
         )
         hand.start()
         if k == 0:
-            each_slab(send_init, n_chip - n_z, n_chip - 1)
+            each_slab(send_init, near_chips)
         spread_own = spread_of(both[0:24])
 
         def operands(spread):
@@ -463,17 +457,16 @@
             for j in range(tiles):
                 piece = pl.ds(pl.multiple_of(b * width + j * 128, 128), 128)
                 vol_c[:, piece] = vol_c[:, piece] + wgt_c[:, piece] * back[j]
-            vol_f[b] = vol_f[b] + wgt_f[b] * back[tiles]
+            packed = vol_f[b] + wgt_f[b] * back[tiles]
             if k < ITERS - 1:
+                vol_f[b] = packed
                 acc = add_moment(b, acc)
+            else:
+                for j in range(tiles):
+                    piece = pl.ds(pl.multiple_of(b * width + j * 128, 128), 128)
+                    fine_out[:, piece] = packed[j * rows_f : (j + 1) * rows_f]
         if k < ITERS - 1:
             finish_moment(k + 1, acc)
-
-    coarse_out[...] = vol_c[...]
-    for b in range(n_view):
-        for j in range(tiles):
-            part = slice(b * width + j * 128, b * width + (j + 1) * 128)
-            fine_out[:, part] = vol_f[b, j * rows_f : (j + 1) * rows_f, :]
 
     others(init_all, init_send_sem.at[0], init_recv_sem.at[0], n_slab - 2).wait_send()
     init_hand.wait_send()
@@ -482,7 +475,7 @@
     for k in range(ITERS):
         if k > 0:
             others(
-                moment_all.at[k], moment_send_sem.at[k], moment_recv_sem.at[k], n_slab - 1
+                moment_all.at[k], moment_send_sem.at[k], moment_recv_sem.at[k, 0], n_slab - 1
             ).wait_send()
         to_slab(
             spread_send.at[k], spread_recv.at[k], spread_send_sem.at[k], spread_recv_sem.at[k], partner
@@ -537,7 +530,6 @@
                 pltpu.VMEM((n_view, 16, 128), F32),
                 pltpu.VMEM((n_view, 16, 128), F32),
                 pltpu.VMEM((rows_c, cells), F32),
-                pltpu.VMEM((rows_c, cells), F32),
                 pltpu.VMEM((2, 7, 8, 128), BF16),
                 pltpu.VMEM((n_slab, 7, 8, 128), BF16),
                 pltpu.VMEM((all_w, n_slab * 24), BF16),
@@ -564,7 +556,7 @@
                 dma((2,)),
                 dma((2,)),
                 dma((ITERS,)),
-                dma((ITERS,)),
+                dma((ITERS, 2)),
                 dma((ITERS,)),
                 dma((ITERS,)),
                 dma((ITERS,)),

time: 73.2 us -> 73.1 us (level)
  no operation moved by 1% of the time
where the time goes in v5:
time: 73.1 us; the launch traced here: 73 us
  Pallas kernels  72.3 us (99%)
    pallas_call x1, Pallas kernels, body(): pl.pallas_call(functools.partial(kernel, n_z, n_y, n_slab, n_view), name=...  71.6 us

profile of v5, /device:TPU:1, one launch (start us, length us, event | category | flops | bytes accessed | tf_op | source)
XLA Modules:
  0.0 73.0 jit_solution(11770710573244858037)
XLA Ops:
  0.6 71.6 %sirt.1 = (f32[4,4096]{1,0:T(4,128)S(1)}, f32[16,4096]{1,0:T(8,128)S(1)}) custom-call(f32[4,4096]{1,0:T(4,128)} %fine_volume.1, f32[16,4096]{1,0:T(8,128)} %coarse_volume.1, bf16[2,4096,128]{2,1,0:T(8,128)(2,1)} %fine_rays.1, bf16[2,4096,128]{2,1,0:T(8,128)(2,1)} %coarse_rays.1, bf16[2,4,256]{2,1,0:T(4,128)(2,1)} %fine_axial.1, ...), custom_call_target="tpu_custom_call" | custom-call | tf_op jit(solution)/shard_map/sirt/pallas_call | solution.py:514
  72.2 0.7 %put_out.1 = (f32[4,4096]{1,0:T(4,128)}, f32[16,4096]{1,0:T(8,128)}) custom-call(f32[4,4096]{1,0:T(4,128)S(1)} %get-tuple-element.4.fine, f32[16,4096]{1,0:T(8,128)S(1)} %get-tuple-element.5.coarse), custom_call_target="tpu_custom_call" | custom-call | tf_op jit(solution)/shard_map/put_out/pallas_call | solution.py:569

commit v6 on v5

--- a/solution.py
+++ b/solution.py
@@ -340,6 +340,9 @@
         key=lambda p: -(p[0] + min(p[1], n_y - p[1])),
     )
 
+    hops = [lambda p, h=h: p[0] + min(p[1], n_y - p[1]) == h for h in range(n_y // 2 + n_xlo)]
+    groups = [[p for p in view_order if same(p)] for same in hops]
+
     def view_of(step):
         dx, dy = step
         return lax.rem(x_lo + dx, n_xlo) * n_y + lax.rem(y + dy, n_y)
@@ -407,11 +410,8 @@
             back_own[i, :, width : width + 128] = term_f
         hand.wait_recv()
         other_c, other_f = operands(spread_recv[k].reshape(24, 128))
-        for i, step in enumerate(view_order):
+        def hand_out(step, term_c, term_f):
             b = view_of(step)
-            term_c, term_f = terms(other_c, other_f, 1 - core, b)
-            term_c = term_c + back_own[i, :, 0:width]
-            term_f = term_f + back_own[i, :, width : width + 128]
             dest = back_recv.at[k, view] if step == (0, 0) else back_send.at[k, b]
             for j in range(tiles):
                 dest[j] = term_c[:, j * 128 : (j + 1) * 128].astype(BF16)
@@ -424,6 +424,16 @@
                     back_recv_sem.at[k, view],
                     b,
                 ).start()
+
+        ready = None
+        for i, step in enumerate(view_order):
+            term_c, term_f = terms(other_c, other_f, 1 - core, view_of(step))
+            if ready is not None:
+                hand_out(*ready)
+            term_c = term_c + back_own[i, :, 0:width]
+            term_f = term_f + back_own[i, :, width : width + 128]
+            ready = (step, term_c, term_f)
+        hand_out(*ready)
         total = back_recv[k, view].astype(F32)
         for step in reversed(view_order):
             if step == (0, 0):
@@ -445,26 +455,27 @@
                 view_of(step),
             ).start()
         acc = zero
-        for step in reversed(view_order):
-            b = view_of(step)
-            if step == (0, 0):
-                back = sum_send[k].astype(F32)
-            else:
-                to_view(
-                    sum_send.at[k], sum_recv.at[k, b], sum_send_sem.at[k], sum_recv_sem.at[k, b], b
-                ).wait_recv()
-                back = sum_recv[k, b].astype(F32)
-            for j in range(tiles):
-                piece = pl.ds(pl.multiple_of(b * width + j * 128, 128), 128)
-                vol_c[:, piece] = vol_c[:, piece] + wgt_c[:, piece] * back[j]
-            packed = vol_f[b] + wgt_f[b] * back[tiles]
-            if k < ITERS - 1:
-                vol_f[b] = packed
-                acc = add_moment(b, acc)
-            else:
+        for group in groups:
+            for step in group:
+                if step != (0, 0):
+                    b = view_of(step)
+                    to_view(
+                        sum_send.at[k], sum_recv.at[k, b], sum_send_sem.at[k], sum_recv_sem.at[k, b], b
+                    ).wait_recv()
+            for step in group:
+                b = view_of(step)
+                back = (sum_send[k] if step == (0, 0) else sum_recv[k, b]).astype(F32)
                 for j in range(tiles):
                     piece = pl.ds(pl.multiple_of(b * width + j * 128, 128), 128)
-                    fine_out[:, piece] = packed[j * rows_f : (j + 1) * rows_f]
+                    vol_c[:, piece] = vol_c[:, piece] + wgt_c[:, piece] * back[j]
+                packed = vol_f[b] + wgt_f[b] * back[tiles]
+                if k < ITERS - 1:
+                    vol_f[b] = packed
+                    acc = add_moment(b, acc)
+                else:
+                    for j in range(tiles):
+                        piece = pl.ds(pl.multiple_of(b * width + j * 128, 128), 128)
+                        fine_out[:, piece] = packed[j * rows_f : (j + 1) * rows_f]
         if k < ITERS - 1:
             finish_moment(k + 1, acc)
 

time: 73.1 us -> 71.5 us (0.978)
  Pallas kernels: 72.3 us -> 70.8 us
    pallas_call x1, Pallas kernels: 71.6 us -> 70 us  [body(): pl.pallas_call(functools.partial(kernel, n_z, n_y, n_slab, n_view), name=...]
where the time goes in v6:
time: 71.5 us; the launch traced here: 71.4 us
  Pallas kernels  70.8 us (99%)
    pallas_call x1, Pallas kernels, body(): pl.pallas_call(functools.partial(kernel, n_z, n_y, n_slab, n_view), name=...  70 us

profile of v6, /device:TPU:1, one launch (start us, length us, event | category | flops | bytes accessed | tf_op | source)
XLA Modules:
  0.0 71.4 jit_solution(7168489711631572860)
XLA Ops:
  0.6 70.0 %sirt.1 = (f32[4,4096]{1,0:T(4,128)S(1)}, f32[16,4096]{1,0:T(8,128)S(1)}) custom-call(f32[4,4096]{1,0:T(4,128)} %fine_volume.1, f32[16,4096]{1,0:T(8,128)} %coarse_volume.1, bf16[2,4096,128]{2,1,0:T(8,128)(2,1)} %fine_rays.1, bf16[2,4096,128]{2,1,0:T(8,128)(2,1)} %coarse_rays.1, bf16[2,4,256]{2,1,0:T(4,128)(2,1)} %fine_axial.1, ...), custom_call_target="tpu_custom_call" | custom-call | tf_op jit(solution)/shard_map/sirt/pallas_call | solution.py:525
  70.7 0.7 %put_out.1 = (f32[4,4096]{1,0:T(4,128)}, f32[16,4096]{1,0:T(8,128)}) custom-call(f32[4,4096]{1,0:T(4,128)S(1)} %get-tuple-element.4.fine, f32[16,4096]{1,0:T(8,128)S(1)} %get-tuple-element.5.coarse), custom_call_target="tpu_custom_call" | custom-call | tf_op jit(solution)/shard_map/put_out/pallas_call | solution.py:580

commit v7 on v6

--- a/solution.py
+++ b/solution.py
@@ -384,8 +384,6 @@
             spread_send.at[k], spread_recv.at[k], spread_send_sem.at[k], spread_recv_sem.at[k], partner
         )
         hand.start()
-        if k == 0:
-            each_slab(send_init, near_chips)
         spread_own = spread_of(both[0:24])
 
         def operands(spread):
@@ -434,6 +432,8 @@
             term_f = term_f + back_own[i, :, width : width + 128]
             ready = (step, term_c, term_f)
         hand_out(*ready)
+        if k == 0:
+            each_slab(send_init, near_chips)
         total = back_recv[k, view].astype(F32)
         for step in reversed(view_order):
             if step == (0, 0):

time: 71.5 us -> 71.7 us (level)
  no operation moved by 1% of the time
where the time goes in v7:
time: 71.7 us; the launch traced here: 71.6 us
  Pallas kernels  71 us (99%)
    pallas_call x1, Pallas kernels, body(): pl.pallas_call(functools.partial(kernel, n_z, n_y, n_slab, n_view), name=...  70.3 us

profile of v7, /device:TPU:1, one launch (start us, length us, event | category | flops | bytes accessed | tf_op | source)
XLA Modules:
  0.0 71.6 jit_solution(12435529797549590940)
XLA Ops:
  0.6 70.3 %sirt.1 = (f32[4,4096]{1,0:T(4,128)S(1)}, f32[16,4096]{1,0:T(8,128)S(1)}) custom-call(f32[4,4096]{1,0:T(4,128)} %fine_volume.1, f32[16,4096]{1,0:T(8,128)} %coarse_volume.1, bf16[2,4096,128]{2,1,0:T(8,128)(2,1)} %fine_rays.1, bf16[2,4096,128]{2,1,0:T(8,128)(2,1)} %coarse_rays.1, bf16[2,4,256]{2,1,0:T(4,128)(2,1)} %fine_axial.1, ...), custom_call_target="tpu_custom_call" | custom-call | tf_op jit(solution)/shard_map/sirt/pallas_call | solution.py:525
  70.9 0.7 %put_out.1 = (f32[4,4096]{1,0:T(4,128)}, f32[16,4096]{1,0:T(8,128)}) custom-call(f32[4,4096]{1,0:T(4,128)S(1)} %get-tuple-element.4.fine, f32[16,4096]{1,0:T(8,128)S(1)} %get-tuple-element.5.coarse), custom_call_target="tpu_custom_call" | custom-call | tf_op jit(solution)/shard_map/put_out/pallas_call | solution.py:580
